TPU v7x, 256 devices: a whole 4x4x8 slice. The times are simulated.
256 devices in a mesh: outer: 8 (over y, core), inner: 32 (over x, z).
Axes of the slice: x: 4, y: 4, z: 8, core: 2. Of those that a mesh axis runs over, the one named last changes fastest.
Arguments:
- queries: bfloat16 [131072, 16, 128], P(('outer', 'inner')), may hold values from -1.5 to 1.5
- key_vectors: bfloat16 [131072, 16, 128], P(('outer', 'inner')), may hold values from -1.5 to 1.5
- value_vectors: bfloat16 [131072, 16, 128], P(('outer', 'inner')), may hold values from -6 to 6
- level_weights: float32 [18, 16, 131072], P(None, None, ('outer', 'inner')), may hold values from 0.25 to 1
Outputs:
- attended: bfloat16 [131072, 16, 128], P(('outer', 'inner'))
All inputs are finite; a program needn't handle non-finite values.
Results may differ from a plain program's by a relative error of at most 0.0049.
Values may be sent and summed in bfloat16 or wider, within the bound.
A program may use at most 128 MiB of HBM per device.

v0:
```python
import jax
import jax.numpy as jnp
from jax import lax
from jax.sharding import PartitionSpec as P


def swapped(value, axis, distance):
    return lax.ppermute(value, axis, [(i, i ^ 1 << distance) for i in range(lax.axis_size(axis))])


def joined_along(blocks, dim):
    dims = list(blocks.shape[1:])
    dims[dim] *= blocks.shape[0]
    return jnp.moveaxis(blocks, 0, dim).reshape(dims)


def sent_to_all(value, axis):
    copies = jnp.broadcast_to(value, (lax.axis_size(axis), *value.shape))
    return lax.all_to_all(copies, axis, split_axis=0, concat_axis=0, tiled=True)


def gather_directly(value, axis, dim):
    return joined_along(sent_to_all(value, axis), dim)


def level_table(block_len):
    position = jnp.arange(block_len, dtype=jnp.int32)
    differ = position[:, None] ^ position[None, :]
    levels_at = jnp.zeros((block_len, block_len), jnp.int32)
    for bit_pos in range(block_len.bit_length() - 1):
        levels_at = levels_at + (differ >= 1 << bit_pos).astype(jnp.int32)
    causal = position[None, :] <= position[:, None]
    return (levels_at, causal)


def scaled_gains(level_weights):
    count = level_weights.shape[0]
    factor = jnp.exp2(-0.5 * jnp.arange(count, dtype=jnp.float32))
    return level_weights * factor[:, None, None]


def local_terms(queries, key_vectors, value_vectors, gains):
    block_len = queries.shape[0]
    levels_at, causal = level_table(block_len)
    scores = jnp.einsum("thd,shd->hts", queries, key_vectors, preferred_element_type=jnp.float32)
    weighting = jnp.zeros(scores.shape, jnp.float32)
    for level_idx in range(block_len.bit_length()):
        weighting = weighting + jnp.where(
            (levels_at == level_idx)[None], gains[level_idx][:, :, None], jnp.float32(0.0)
        )
    attn_weights = jnp.where(causal[None], scores * weighting, jnp.float32(0.0)).astype(
        jnp.bfloat16
    )
    return jnp.einsum(
        "hts,shd->thd", attn_weights, value_vectors, preferred_element_type=jnp.float32
    )


def sibling_buckets(states, outer_place, outer_depth):
    picked = []
    tier_now = states
    for bit_pos in range(outer_depth):
        sibling = outer_place >> bit_pos ^ 1
        picked.append(
            lax.dynamic_index_in_dim(tier_now, sibling, 0, keepdims=False).astype(jnp.bfloat16)
        )
        if bit_pos + 1 < outer_depth:
            tier_now = tier_now[0::2] + tier_now[1::2]
    return picked


def per_device(queries, key_vectors, value_vectors, level_weights):
    inner_count = lax.axis_size("inner")
    inner_depth = inner_count.bit_length() - 1
    outer_depth = lax.axis_size("outer").bit_length() - 1
    outer_place = lax.axis_index("outer")
    place = outer_place * inner_count + lax.axis_index("inner")
    block_len = queries.shape[0]
    head_count = queries.shape[1]
    head_width = queries.shape[2]
    local_depth = block_len.bit_length() - 1
    gains = scaled_gains(level_weights)
    key_value = jnp.einsum(
        "shd,she->hde", key_vectors, value_vectors, preferred_element_type=jnp.float32
    )
    output_sum = local_terms(queries, key_vectors, value_vectors, gains)
    buckets = []
    running = key_value
    for bit_pos in range(inner_depth):
        partner = swapped(running, "inner", bit_pos)
        buckets.append(partner.astype(jnp.bfloat16))
        running = running + partner
    share = head_count * head_width // inner_count
    share_rows = lax.dynamic_slice_in_dim(
        running.reshape(head_count * head_width, head_width),
        lax.axis_index("inner") * share,
        share,
        0,
    )
    states = lax.all_gather(share_rows[None], "outer", axis=0, tiled=True)
    received = sibling_buckets(states, outer_place, outer_depth)
    collected = gather_directly(jnp.stack(received), "inner", 1)
    for step_idx in range(outer_depth):
        buckets.append(collected[step_idx].reshape(head_count, head_width, head_width))
    count = len(buckets)
    switches = [(place >> bit_pos & 1).astype(jnp.float32) for bit_pos in range(count)]
    for bit_pos in range(count):
        contrib = jnp.einsum(
            "thd,hde->the", queries, buckets[bit_pos], preferred_element_type=jnp.float32
        )
        level_gain = gains[local_depth + 1 + bit_pos] * switches[bit_pos]
        output_sum = output_sum + contrib * level_gain.T[:, :, None]
    return output_sum.astype(jnp.bfloat16)


def solution(mesh):
    placed = (
        P(("outer", "inner"), None, None),
        P(("outer", "inner"), None, None),
        P(("outer", "inner"), None, None),
        P(None, None, ("outer", "inner")),
    )
    return jax.shard_map(
        per_device,
        mesh=mesh,
        in_specs=placed,
        out_specs=P(("outer", "inner"), None, None),
        check_vma=False,
    )
```

profile of v0, /device:TPU:8, one launch (start us, length us, event | category | flops | bytes accessed | tf_op | source)
XLA Modules:
  0.0 270.3 jit_solution(13188001919686625349)
XLA Ops:
  0.0 0.0 copy-start
  0.0 4.4 %copy.61 = bf16[512,16,128]{0,2,1:T(8,128)(2,1)} copy(bf16[512,16,128]{2,1,0:T(8,128)(2,1)} %param.5) | data formatting | bytes 4194304 | tf_op args[1]
  4.4 0.0 copy-done
  4.4 2.7 %fusion.10 = f32[16,128,128]{2,1,0:T(8,128)S(1)} fusion(bf16[512,16,128]{0,2,1:T(8,128)(2,1)} %copy.61, bf16[512,16,128]{2,1,0:T(8,128)(2,1)S(1)} %copy-done), kind=kOutput, calls=%fused_computation.19 | convolution fusion | flops 268435456 | bytes 5242880 | tf_op jit(solution)/shard_map/shd,she->hde/dot_general | solution.py:83
  7.2 2.0 collective-permute-start
  9.2 23.2 %collective-permute-done = f32[16,128,128]{2,1,0:T(8,128)S(1)} collective-permute-done((f32[16,128,128]{2,1,0:T(8,128)S(1)}, f32[16,128,128]{2,1,0:T(8,128)S(1)}, u32[]{:S(2)}, u32[]{:S(2)}) %collective-permute-start) | collective-permute-done | bytes 1048608 | tf_op jit(solution)/shard_map/ppermute | solution.py:8
  32.3 0.1 add.525
  32.5 3.4 %collective-permute-start.1 = (f32[16,128,128]{2,1,0:T(8,128)S(1)}, f32[16,128,128]{2,1,0:T(8,128)S(1)}, u32[]{:S(2)}, u32[]{:S(2)}) collective-permute-start(f32[16,128,128]{2,1,0:T(8,128)S(1)} %add.525), channel_id=1, source_target_pairs={{0,2},{1,3},{2,0},{3,1},{4,6},{5,7},{6,4},{7,5},{8,10},{9,11},{10,... | collective-permute-start | bytes 3145736 | tf_op jit(solution)/shard_map/ppermute | solution.py:8
  35.8 44.9 %collective-permute-done.1 = f32[16,128,128]{2,1,0:T(8,128)S(1)} collective-permute-done((f32[16,128,128]{2,1,0:T(8,128)S(1)}, f32[16,128,128]{2,1,0:T(8,128)S(1)}, u32[]{:S(2)}, u32[]{:S(2)}) %collective-permute-start.1) | collective-permute-done | bytes 1048608 | tf_op jit(solution)/shard_map/ppermute | solution.py:8
  80.8 0.1 add.527
  80.9 6.3 %collective-permute-start.2 = (f32[16,128,128]{2,1,0:T(8,128)S(1)}, f32[16,128,128]{2,1,0:T(8,128)S(1)}, u32[]{:S(2)}, u32[]{:S(2)}) collective-permute-start(f32[16,128,128]{2,1,0:T(8,128)S(1)} %add.527), channel_id=1, source_target_pairs={{0,4},{1,5},{2,6},{3,7},{4,0},{5,1},{6,2},{7,3},{8,12},{9,13},{10,... | collective-permute-start | bytes 3145736 | tf_op jit(solution)/shard_map/ppermute | solution.py:8
  87.2 45.8 %collective-permute-done.2 = f32[16,128,128]{2,1,0:T(8,128)S(1)} collective-permute-done((f32[16,128,128]{2,1,0:T(8,128)S(1)}, f32[16,128,128]{2,1,0:T(8,128)S(1)}, u32[]{:S(2)}, u32[]{:S(2)}) %collective-permute-start.2) | collective-permute-done | bytes 1048608 | tf_op jit(solution)/shard_map/ppermute | solution.py:8
  133.0 0.1 add.529
  133.2 1.6 collective-permute-start.3
  134.7 1.1 broadcast_compare_fusion.7
  135.8 1.1 broadcast_compare_fusion.5
  136.9 1.2 broadcast_compare_fusion.3
  138.1 1.1 broadcast_compare_fusion.1
  139.2 0.0 copy-done.8
  139.2 18.0 %collective-permute-done.3 = f32[16,128,128]{2,1,0:T(8,128)S(1)} collective-permute-done((f32[16,128,128]{2,1,0:T(8,128)S(1)}, f32[16,128,128]{2,1,0:T(8,128)S(1)}, u32[]{:S(2)}, u32[]{:S(2)}) %collective-permute-start.3) | collective-permute-done | bytes 1048608 | tf_op jit(solution)/shard_map/ppermute | solution.py:8
  157.2 1.3 add.531
  158.5 0.0 copy-done.10
  158.5 3.0 %collective-permute-start.4 = (f32[16,128,128]{2,1,0:T(8,128)}, f32[16,128,128]{2,1,0:T(8,128)}, u32[]{:S(2)}, u32[]{:S(2)}) collective-permute-start(f32[16,128,128]{2,1,0:T(8,128)} %add.531), channel_id=1, source_target_pairs={{0,16},{1,17},{2,18},{3,19},{4,20},{5,21},{6,22},{7,23},{8,24},{9,... | collective-permute-start | bytes 3145736 | tf_op jit(solution)/shard_map/ppermute | solution.py:8
  161.5 0.0 copy-done.12
  161.5 1.0 broadcast_compare_fusion.9
  162.5 1.1 iota_compare_fusion
  163.7 1.2 broadcast_multiply_fusion
  164.8 0.7 slice_bitcast_fusion.9
  165.6 0.7 fusion.52
  166.3 17.2 %collective-permute-done.4 = f32[16,128,128]{2,1,0:T(8,128)} collective-permute-done((f32[16,128,128]{2,1,0:T(8,128)}, f32[16,128,128]{2,1,0:T(8,128)}, u32[]{:S(2)}, u32[]{:S(2)}) %collective-permute-start.4) | collective-permute-done | bytes 1048608 | tf_op jit(solution)/shard_map/ppermute | solution.py:8
  183.5 1.7 add.533
  185.1 13.1 %all-gather = f32[512,128]{1,0:T(8,128)S(1)} all-gather(f32[64,128]{1,0:T(8,128)S(1)} %constant_dynamic-slice_fusion), channel_id=2, replica_groups=mesh['outer'=8,'inner'=32] {'outer'}, dimensions={0}, use_global_device_ids=true | all-gather | bytes 294912 | tf_op jit(solution)/shard_map/all_gather | solution.py:100
  198.3 1.5 broadcast_in_dim.212
  199.9 8.8 %all-to-all-start = ((bf16[32,3,64,128]{3,2,1,0:T(8,128)(2,1)}), bf16[32,3,64,128]{3,2,1,0:T(8,128)(2,1)}, u32[]{:S(2)}, u32[]{:S(2)}) async-start(bf16[32,3,64,128]{3,2,1,0:T(8,128)(2,1)} %broadcast_in_dim.212), calls=%async_computation | async-start | bytes 3145728 | tf_op jit(solution)/shard_map/all_to_all | solution.py:19
  208.7 23.0 %select_convert_fusion.clone.4 = bf16[16,512,512]{2,1,0:T(8,128)(2,1)S(1)} fusion(bf16[512,16,128]{0,2,1:T(8,128)(2,1)} %copy.61, f32[16,512]{1,0:T(8,128)} %get-tuple-element.16, f32[16,512]{1,0:T(8,128)} %get-tuple-element.17, f32[16,512]{1,0:T(8,128)} %get-tuple-element.18, f32[16,512]{1,0:T(8,128)} %get-tuple-element.20, ...), kind=kOutput, calls=%fused_computation.clone.clone.clone.1 | convolution fusion | flops 1166016512 | bytes 15794176 | tf_op jit(solution)/shard_map/thd,shd->hts/dot_general | solution.py:45
  231.6 0.0 copy-start.1
  231.7 4.3 %fusion.9 = f32[16,512,128]{2,1,0:T(8,128)} fusion(bf16[512,16,128]{2,1,0:T(8,128)(2,1)S(1)} %copy-done, bf16[16,512,512]{2,1,0:T(8,128)(2,1)S(1)} %select_convert_fusion.clone.4), kind=kOutput, calls=%fused_computation.18 | convolution fusion | flops 1073741824 | bytes 14680064 | tf_op jit(solution)/shard_map/hts,shd->thd/dot_general | solution.py:54
  236.0 0.0 copy-done.1
  236.0 2.7 %fusion.29 = f32[16,128,512]{1,2,0:T(8,128)} fusion(f32[16,128,128]{2,1,0:T(8,128)S(1)} %collective-permute-done, bf16[512,16,128]{2,1,0:T(8,128)(2,1)S(1)} %copy-done.1), kind=kOutput, calls=%fused_computation.42 | convolution fusion | flops 268697600 | bytes 7340032 | tf_op jit(solution)/shard_map/thd,hde->the/dot_general | solution.py:108
  238.7 0.0 copy-done.9
  238.7 2.7 %fusion.27 = f32[16,128,512]{1,2,0:T(8,128)} fusion(f32[16,128,128]{2,1,0:T(8,128)S(1)} %copy-done.9, bf16[512,16,128]{2,1,0:T(8,128)(2,1)S(1)} %copy-done.1), kind=kOutput, calls=%fused_computation.40 | convolution fusion | flops 268697600 | bytes 7340032 | tf_op jit(solution)/shard_map/thd,hde->the/dot_general | solution.py:108
  241.4 0.0 copy-done.11
  241.4 2.7 fusion.25
  244.1 0.0 copy-done.13
  244.1 2.7 fusion.23
  246.8 1.4 all-to-all-done
  248.2 1.7 copy.133
  249.9 0.0 copy-start.7
  249.9 0.1 fusion.54
  250.0 0.2 copy-done.2
  250.3 0.7 fusion.40
  251.0 0.0 copy-start.4
  251.0 0.0 copy-start.5
  251.0 0.7 fusion.36
  251.7 0.0 copy-start.3
  251.7 0.0 copy-start.14
  251.7 0.0 copy-start.15
  251.8 0.7 fusion.38
  252.5 0.9 copy-done.6
  253.4 1.4 copy-done.4
  254.7 1.2 copy-done.5
  255.9 1.2 copy-done.3
  257.1 10.5 %fusion.1 = bf16[512,16,128]{2,0,1:T(8,128)(2,1)S(1)} fusion(f32[16,128,512]{1,2,0:T(8,128)S(1)} %fusion.40, f32[16,128,512]{1,2,0:T(8,128)S(1)} %fusion.38, f32[16,128,512]{1,2,0:T(8,128)S(1)} %fusion.36, f32[16,128,512]{1,2,0:T(8,128)S(1)} %copy-done.7, f32[16,128,512]{1,2,0:T(8,128)S(1)} %copy-done.6, f32[16,128,512]{1,2,0:T(8,128)S(1)} %copy-done.5, ...), kind=kOutput, calls=%fused_computation.3 | convolution fusion | flops 286523392 | bytes 39059456 | tf_op jit(solution)/shard_map/thd,hde->the/dot_general | solution.py:108
  267.6 2.7 copy.88
  (18 shorter events, 0.1 us)
Async XLA Ops:
  0.0 4.4 %copy-start = (bf16[512,16,128]{2,1,0:T(8,128)(2,1)S(1)}, bf16[512,16,128]{2,1,0:T(8,128)(2,1)}, u32[]{:S(2)}) copy-start(bf16[512,16,128]{2,1,0:T(8,128)(2,1)} %param.6) | copy-start | bytes 6291460
  7.2 25.2 %collective-permute-start = (f32[16,128,128]{2,1,0:T(8,128)S(1)}, f32[16,128,128]{2,1,0:T(8,128)S(1)}, u32[]{:S(2)}, u32[]{:S(2)}) collective-permute-start(f32[16,128,128]{2,1,0:T(8,128)S(1)} %fusion.10), channel_id=1, source_target_pairs={{0,1},{1,0},{2,3},{3,2},{4,5},{5,4},{6,7},{7,6},{8,9},{9,8},{10,11... | collective-permute-start | bytes 3145736 | tf_op jit(solution)/shard_map/ppermute | solution.py:8
  32.5 48.3 %collective-permute-start.1 = (f32[16,128,128]{2,1,0:T(8,128)S(1)}, f32[16,128,128]{2,1,0:T(8,128)S(1)}, u32[]{:S(2)}, u32[]{:S(2)}) collective-permute-start(f32[16,128,128]{2,1,0:T(8,128)S(1)} %add.525), channel_id=1, source_target_pairs={{0,2},{1,3},{2,0},{3,1},{4,6},{5,7},{6,4},{7,5},{8,10},{9,11},{10,... | collective-permute-start | bytes 3145736 | tf_op jit(solution)/shard_map/ppermute | solution.py:8
  80.8 58.5 %copy-start.8 = (f32[16,128,128]{2,1,0:T(8,128)}, f32[16,128,128]{2,1,0:T(8,128)S(1)}, u32[]{:S(2)}) copy-start(f32[16,128,128]{2,1,0:T(8,128)S(1)} %collective-permute-done.1) | copy-start | bytes 3145732
  80.9 52.1 %collective-permute-start.2 = (f32[16,128,128]{2,1,0:T(8,128)S(1)}, f32[16,128,128]{2,1,0:T(8,128)S(1)}, u32[]{:S(2)}, u32[]{:S(2)}) collective-permute-start(f32[16,128,128]{2,1,0:T(8,128)S(1)} %add.527), channel_id=1, source_target_pairs={{0,4},{1,5},{2,6},{3,7},{4,0},{5,1},{6,2},{7,3},{8,12},{9,13},{10,... | collective-permute-start | bytes 3145736 | tf_op jit(solution)/shard_map/ppermute | solution.py:8
  133.0 25.5 %copy-start.10 = (f32[16,128,128]{2,1,0:T(8,128)}, f32[16,128,128]{2,1,0:T(8,128)S(1)}, u32[]{:S(2)}) copy-start(f32[16,128,128]{2,1,0:T(8,128)S(1)} %collective-permute-done.2) | copy-start | bytes 3145732
  133.2 24.1 %collective-permute-start.3 = (f32[16,128,128]{2,1,0:T(8,128)S(1)}, f32[16,128,128]{2,1,0:T(8,128)S(1)}, u32[]{:S(2)}, u32[]{:S(2)}) collective-permute-start(f32[16,128,128]{2,1,0:T(8,128)S(1)} %add.529), channel_id=1, source_target_pairs={{0,8},{1,9},{2,10},{3,11},{4,12},{5,13},{6,14},{7,15},{8,0},{9,1},... | collective-permute-start | bytes 3145736 | tf_op jit(solution)/shard_map/ppermute | solution.py:8
  157.2 4.3 %copy-start.12 = (f32[16,128,128]{2,1,0:T(8,128)}, f32[16,128,128]{2,1,0:T(8,128)S(1)}, u32[]{:S(2)}) copy-start(f32[16,128,128]{2,1,0:T(8,128)S(1)} %collective-permute-done.3) | copy-start | bytes 3145732
  158.5 25.0 %collective-permute-start.4 = (f32[16,128,128]{2,1,0:T(8,128)}, f32[16,128,128]{2,1,0:T(8,128)}, u32[]{:S(2)}, u32[]{:S(2)}) collective-permute-start(f32[16,128,128]{2,1,0:T(8,128)} %add.531), channel_id=1, source_target_pairs={{0,16},{1,17},{2,18},{3,19},{4,20},{5,21},{6,22},{7,23},{8,24},{9,... | collective-permute-start | bytes 3145736 | tf_op jit(solution)/shard_map/ppermute | solution.py:8
  199.9 48.3 %all-to-all-start = ((bf16[32,3,64,128]{3,2,1,0:T(8,128)(2,1)}), bf16[32,3,64,128]{3,2,1,0:T(8,128)(2,1)}, u32[]{:S(2)}, u32[]{:S(2)}) async-start(bf16[32,3,64,128]{3,2,1,0:T(8,128)(2,1)} %broadcast_in_dim.212), calls=%async_computation | async-start | bytes 3145728 | tf_op jit(solution)/shard_map/all_to_all | solution.py:19
  231.6 4.3 %copy-start.1 = (bf16[512,16,128]{2,1,0:T(8,128)(2,1)S(1)}, bf16[512,16,128]{2,1,0:T(8,128)(2,1)}, u32[]{:S(2)}) copy-start(bf16[512,16,128]{2,1,0:T(8,128)(2,1)} %param.4) | copy-start | bytes 6291460
  236.0 2.7 %copy-start.9 = (f32[16,128,128]{2,1,0:T(8,128)S(1)}, f32[16,128,128]{2,1,0:T(8,128)}, u32[]{:S(2)}) copy-start(f32[16,128,128]{2,1,0:T(8,128)} %copy-done.8) | copy-start | bytes 3145732
  238.7 2.7 %copy-start.11 = (f32[16,128,128]{2,1,0:T(8,128)S(1)}, f32[16,128,128]{2,1,0:T(8,128)}, u32[]{:S(2)}) copy-start(f32[16,128,128]{2,1,0:T(8,128)} %copy-done.10) | copy-start | bytes 3145732
  241.4 2.7 copy-start.13
  248.2 2.1 copy-start.2
  249.9 2.6 copy-start.7
  250.3 3.1 %copy-start.6 = (f32[16,128,512]{1,2,0:T(8,128)S(1)}, f32[16,128,512]{1,2,0:T(8,128)}, u32[]{:S(2)}) copy-start(f32[16,128,512]{1,2,0:T(8,128)} %fusion.25) | copy-start | bytes 12582916
  251.0 3.8 %copy-start.4 = (f32[16,128,512]{1,2,0:T(8,128)S(1)}, f32[16,128,512]{1,2,0:T(8,128)}, u32[]{:S(2)}) copy-start(f32[16,128,512]{1,2,0:T(8,128)} %fusion.29) | copy-start | bytes 12582916
  251.0 4.9 %copy-start.5 = (f32[16,128,512]{1,2,0:T(8,128)S(1)}, f32[16,128,512]{1,2,0:T(8,128)}, u32[]{:S(2)}) copy-start(f32[16,128,512]{1,2,0:T(8,128)} %fusion.27) | copy-start | bytes 12582916
  251.7 5.4 %copy-start.3 = (f32[16,512,128]{2,1,0:T(8,128)S(1)}, f32[16,512,128]{2,1,0:T(8,128)}, u32[]{:S(2)}) copy-start(f32[16,512,128]{2,1,0:T(8,128)} %fusion.9) | copy-start | bytes 12582916
  251.7 5.4 %copy-start.14 = (f32[512,16]{0,1:T(8,128)S(1)}, f32[512,16]{0,1:T(8,128)}, u32[]{:S(2)}) copy-start(f32[512,16]{0,1:T(8,128)} %get-tuple-element.12) | copy-start | bytes 98308
  251.7 5.4 %copy-start.15 = (f32[512,16]{0,1:T(8,128)S(1)}, f32[512,16]{0,1:T(8,128)}, u32[]{:S(2)}) copy-start(f32[512,16]{0,1:T(8,128)} %get-tuple-element.13) | copy-start | bytes 98308
where the time goes:
time: 271 us; the launch traced here: 270 us
  waiting for transfers between devices  151 us (56%)
  matrix products  53.4 us (20%)
  starting transfers between devices  25.1 us (9%)
  local copies, waits for them, and re-layouts  16.1 us (6%)
  blocking collectives  13.1 us (5%)
  other arithmetic  11.8 us (4%)
    ppermute x5, waiting for transfers between devices, swapped(): lax.ppermute(value, axis, [(i, i ^ 1 << distance) for i in range(lax.axis...  149 us
    dot_general x8, matrix products, per_device(): jnp.einsum('thd,hde->the', queries, buckets[bit_pos], preferred_element_t...  23.4 us
    dot_general x1, matrix products, local_terms(): jnp.einsum('thd,shd->hts', queries, key_vectors, preferred_element_type=j...  23 us
    ppermute x5, starting transfers between devices, swapped(): lax.ppermute(value, axis, [(i, i ^ 1 << distance) for i in range(lax.axis...  16.3 us
    all_gather x1, blocking collectives, per_device(): states = lax.all_gather(share_rows[None], 'outer', axis=0, tiled=True)  13.1 us
    unnamed x33, local copies, waits for them, and re-layouts  9.34 us
    all_to_all x1, starting transfers between devices, sent_to_all(): return lax.all_to_all(copies, axis, split_axis=0, concat_axis=0, tiled=True)  8.79 us
    eq x5, other arithmetic, local_terms(): levels_at == level_idx  5.45 us
  transfers between devices with their start and end apart: 6, of which 6 were waited for; matrix products, arithmetic and copies ran while one was open for 18% of the time, Pallas kernels for 0%

commit v1 on v0

v1 whole, which is shorter than its diff:
```python
import math

import jax
import jax.numpy as jnp
from jax import lax
from jax.experimental import pallas as pl
from jax.experimental.pallas import tpu as pltpu
from jax.sharding import PartitionSpec as P

MESH = pl.DeviceIdType.MESH
F32 = jnp.float32
BF16 = jnp.bfloat16

T = 512
H = 16
D = 128
TIERS = 8
LEVELS = 18
LOCAL_BITS = 9
TILE = 128
HOP = 2
DELAY = [HOP * tier for tier in range(TIERS + 1)]
TICKS = H + DELAY[TIERS]
FACTOR = [2.0 ** (-0.5 * level) for level in range(LEVELS)]


def dot_nt(a, b):
    return lax.dot_general(a, b, (((1,), (1,)), ((), ())), preferred_element_type=F32)


def dot_nn(a, b):
    return lax.dot_general(a, b, (((1,), (0,)), ((), ())), preferred_element_type=F32)


def either(value, *options):
    found = value == options[0]
    for option in options[1:]:
        found = jnp.logical_or(found, value == option)
    return found


def kernel(
    q_hbm, k_hbm, v_hbm, lw_hbm, o_hbm,
    x_in, k_in, v_in, lw, q32, k32, v32, qh, kh, vt, wt, acc, outs,
    run, sent, got, in_sem, out_sem, send_sem, extra_sem, recv_sem,
):
    outer = lax.axis_index("outer")
    inner = lax.axis_index("inner")
    core = lax.rem(outer, 2)
    y = lax.div(outer, 2)
    z = lax.rem(inner, 8)
    x = lax.div(inner, 8)
    p = lax.rem(z, 4)
    place = outer * 32 + inner

    copies = [
        pltpu.make_async_copy(k_hbm, k_in, in_sem.at[0]),
        pltpu.make_async_copy(v_hbm, v_in, in_sem.at[1]),
        pltpu.make_async_copy(lw_hbm, lw, in_sem.at[2]),
        pltpu.make_async_copy(q_hbm, x_in, in_sem.at[3]),
    ]
    for copy in copies:
        copy.start()

    def flip(value):
        return value + 1 - 2 * lax.rem(value, 2)

    def at(zz, xx, yy, cc):
        return (yy * 2 + cc, xx * 8 + zz)

    base4 = z - p
    source1 = base4 + jnp.where(p < 2, 2, 1)
    second1 = base4 + jnp.where(p == 1, 3, 0)
    serves1 = either(p, 1, 2)
    source2 = jnp.where(either(z, 0, 1), 7, jnp.where(either(z, 6, 7), 0, jnp.where(either(z, 2, 3), 4, 3)))
    second2 = jnp.where(z == 0, 6, jnp.where(z == 7, 1, jnp.where(z == 3, 5, 2)))
    serves2 = either(z, 0, 3, 4, 7)

    partner = [
        at(flip(z), x, y, core),
        at(source1, x, y, core),
        at(source2, x, y, core),
        at(z, flip(x), y, core),
        at(z, 3 - x, y, core),
        at(z, x, y, 1 - core),
        at(z, x, flip(y), core),
        at(z, x, 3 - y, core),
    ]
    second = {1: at(second1, x, y, core), 2: at(second2, x, y, core)}
    serves = {1: serves1, 2: serves2}

    barrier = pltpu.get_barrier_semaphore()
    for tier in range(TIERS):
        pl.semaphore_signal(barrier, inc=1, device_id=partner[tier], device_id_type=MESH)
    for tier in (1, 2):
        @pl.when(serves[tier])
        def _(tier=tier):
            pl.semaphore_signal(barrier, inc=1, device_id=second[tier], device_id_type=MESH)

    def send(tier, c, device, sem):
        return pltpu.make_async_remote_copy(
            src_ref=sent.at[tier, c],
            dst_ref=got.at[tier, c],
            send_sem=sem,
            recv_sem=recv_sem.at[tier, c],
            device_id=device,
            device_id_type=MESH,
        )

    def start_sends(tier, c):
        if tier in serves:
            @pl.when(serves[tier])
            def _():
                send(tier, c, partner[tier], send_sem.at[tier]).start()
                send(tier, c, second[tier], extra_sem.at[tier]).start()
        else:
            send(tier, c, partner[tier], send_sem.at[tier]).start()

    def widen(source, target):
        def step(i, carry):
            rows = source[pl.ds(i * 32, 32)].astype(F32).reshape(32 * H, D)
            target[pl.ds(pl.multiple_of(i * 32 * H, 32 * H), 32 * H), :] = rows
            return carry
        lax.fori_loop(0, T // 32, step, 0)

    def head_of(source, c):
        return source[pl.ds(c, T, stride=H), :].astype(BF16)

    copies[0].wait()
    widen(k_in, k32)
    copies[1].wait()
    widen(v_in, v32)
    wt[pl.ds(TILE, TILE), pl.ds(0, TILE)] = jnp.zeros((TILE, TILE), BF16)
    wt[pl.ds(3 * TILE, TILE), pl.ds(2 * TILE, TILE)] = jnp.zeros((TILE, TILE), BF16)

    waits = 8 + serves1.astype(jnp.int32) + serves2.astype(jnp.int32)
    pl.semaphore_wait(barrier, waits)

    lane = lax.rem(lax.broadcasted_iota(jnp.int32, (16, T), 1), TILE)
    group = lax.broadcasted_iota(jnp.int32, (16, T), 0)
    coarse = lax.shift_right_logical(lane, 3)
    coarse_diff = jnp.bitwise_xor(coarse, group)
    low_lane = lax.rem(lax.broadcasted_iota(jnp.int32, (8, T), 1), 8)
    low_row = lax.broadcasted_iota(jnp.int32, (8, T), 0)
    low_diff = jnp.bitwise_xor(low_lane, low_row)

    def gain(level, c):
        return lw[level, pl.ds(c, 1), :] * FACTOR[level]

    def local(c):
        q = head_of(q32, c)
        qh[c] = q
        keys = kh[c]
        wide = jnp.zeros((16, T), F32)
        for level in (4, 5, 6, 7):
            wide = jnp.where(coarse_diff >= (1 << (level - 4)), gain(level, c), wide)
        wide = jnp.where(coarse > group, wide, 0.0)
        narrow = jnp.broadcast_to(gain(0, c), (8, T))
        for level in (1, 2, 3):
            narrow = jnp.where(low_diff >= (1 << (level - 1)), gain(level, c), narrow)
        narrow = jnp.where(low_lane >= low_row, narrow, 0.0)
        gain8 = gain(8, c)
        gain9 = gain(9, c)
        shape3 = (16, 8, TILE)
        same = lax.shift_right_logical(lax.broadcasted_iota(jnp.int32, shape3, 2), 3) == lax.broadcasted_iota(
            jnp.int32, shape3, 0
        )
        for j in range(T // TILE):
            scores = dot_nt(keys[j * TILE:(j + 1) * TILE], q[j * TILE:])
            for i in range(j, T // TILE):
                cols = slice(i * TILE, (i + 1) * TILE)
                part = scores[:, (i - j) * TILE:(i - j + 1) * TILE]
                if i == j:
                    weight = jnp.where(
                        same,
                        jnp.broadcast_to(narrow[:, cols].reshape(1, 8, TILE), shape3),
                        jnp.broadcast_to(wide[:, cols].reshape(16, 1, TILE), shape3),
                    ).reshape(TILE, TILE)
                    part = part * weight
                elif i ^ j == 1:
                    part = part * gain8[:, cols]
                else:
                    part = part * gain9[:, cols]
                wt[pl.ds(j * TILE, TILE), pl.ds(i * TILE, TILE)] = part.astype(BF16)
        values = vt[c]
        half = T // 2
        acc[c, :, pl.ds(0, half)] = dot_nn(values[:, :half], wt[pl.ds(0, half), pl.ds(0, half)])
        acc[c, :, pl.ds(half, half)] = dot_nn(values, wt[:, pl.ds(half, half)])

    switches = [
        jnp.bitwise_and(lax.shift_right_logical(place, tier), 1).astype(F32) for tier in range(TIERS)
    ]

    def finish(c):
        half = T // 2
        for part in range(2):
            cols = pl.ds(part * half, half)
            q = qh[c, pl.ds(part * half, half), :]
            total = acc[c, :, cols]
            for tier in range(TIERS):
                row = lw[LOCAL_BITS + 1 + tier, pl.ds(c, 1), cols] * (
                    switches[tier] * FACTOR[LOCAL_BITS + 1 + tier]
                )
                total = total + dot_nt(got[tier, c], q) * row
            outs[c, pl.ds(part * half, half), :] = total.T.astype(BF16)
        pltpu.make_async_copy(outs.at[c], o_hbm.at[c], out_sem.at[c]).start()

    def active(t, tier):
        return jnp.logical_and(t >= DELAY[tier], t < DELAY[tier] + H)

    def tick(t, carry):
        @pl.when(active(t, 0))
        def _():
            keys = head_of(k32, t)
            kh[t] = keys
            values = v32[pl.ds(t, T, stride=H), :].T.astype(BF16)
            vt[t] = values
            state = dot_nn(values, keys)
            run[t] = state
            sent[0, t] = state.astype(BF16)

        for tier in range(1, TIERS):
            @pl.when(active(t, tier))
            def _(tier=tier):
                c = t - DELAY[tier]
                send(tier - 1, c, partner[tier - 1], send_sem.at[tier - 1]).wait_recv()
                total = run[c] + got[tier - 1, c].astype(F32)
                run[c] = total
                sent[tier, c] = total.astype(BF16)

        for tier in range(TIERS):
            @pl.when(active(t, tier))
            def _(tier=tier):
                start_sends(tier, t - DELAY[tier])

        @pl.when(active(t, 0))
        def _():
            @pl.when(t == 0)
            def _():
                copies[2].wait()
                copies[3].wait()
                widen(x_in, q32)
            local(t)

        @pl.when(active(t, TIERS))
        def _():
            c = t - DELAY[TIERS]
            send(TIERS - 1, c, partner[TIERS - 1], send_sem.at[TIERS - 1]).wait_recv()
            finish(c)

        return carry

    lax.fori_loop(0, TICKS, tick, 0)

    def whole(tier, device, sem):
        return pltpu.make_async_remote_copy(
            src_ref=sent.at[tier],
            dst_ref=got.at[tier],
            send_sem=sem,
            recv_sem=recv_sem.at[tier, 0],
            device_id=device,
            device_id_type=MESH,
        )

    for tier in range(TIERS):
        if tier in serves:
            @pl.when(serves[tier])
            def _(tier=tier):
                whole(tier, partner[tier], send_sem.at[tier]).wait_send()
                whole(tier, second[tier], extra_sem.at[tier]).wait_send()
        else:
            whole(tier, partner[tier], send_sem.at[tier]).wait_send()

    def drain(c, carry):
        pltpu.make_async_copy(outs.at[c], o_hbm.at[c], out_sem.at[c]).wait()
        return carry

    lax.fori_loop(0, H, drain, 0)


def per_device(queries, key_vectors, value_vectors, level_weights):
    hbm = pl.BlockSpec(memory_space=pl.ANY)
    by_head = pl.pallas_call(
        kernel,
        out_shape=jax.ShapeDtypeStruct((H, T, D), BF16),
        in_specs=[hbm] * 4,
        out_specs=hbm,
        scratch_shapes=[
            pltpu.VMEM((T, H, D), BF16),
            pltpu.VMEM((T, H, D), BF16),
            pltpu.VMEM((T, H, D), BF16),
            pltpu.VMEM((LEVELS, H, T), F32),
            pltpu.VMEM((T * H, D), F32),
            pltpu.VMEM((T * H, D), F32),
            pltpu.VMEM((T * H, D), F32),
            pltpu.VMEM((H, T, D), BF16),
            pltpu.VMEM((H, T, D), BF16),
            pltpu.VMEM((H, D, T), BF16),
            pltpu.VMEM((T, T), BF16),
            pltpu.VMEM((H, D, T), F32),
            pltpu.VMEM((H, T, D), BF16),
            pltpu.VMEM((H, D, D), F32),
            pltpu.VMEM((TIERS, H, D, D), BF16),
            pltpu.VMEM((TIERS, H, D, D), BF16),
            pltpu.SemaphoreType.DMA((4,)),
            pltpu.SemaphoreType.DMA((H,)),
            pltpu.SemaphoreType.DMA((TIERS,)),
            pltpu.SemaphoreType.DMA((TIERS,)),
            pltpu.SemaphoreType.DMA((TIERS, H)),
        ],
        compiler_params=pltpu.CompilerParams(
            collective_id=0, has_side_effects=True, vmem_limit_bytes=60 * 1024 * 1024
        ),
    )(queries, key_vectors, value_vectors, level_weights)
    return jnp.transpose(by_head, (1, 0, 2))


def solution(mesh):
    placed = (
        P(("outer", "inner"), None, None),
        P(("outer", "inner"), None, None),
        P(("outer", "inner"), None, None),
        P(None, None, ("outer", "inner")),
    )
    return jax.shard_map(
        per_device,
        mesh=mesh,
        in_specs=placed,
        out_specs=P(("outer", "inner"), None, None),
        check_vma=False,
    )
```

time: 271 us -> 74.5 us (0.27)
  waiting for transfers between devices: 151 us -> 0 us
  Pallas kernels: 0 us -> 69.1 us
  matrix products: 53.4 us -> 0 us
  starting transfers between devices: 25.1 us -> 0 us
  blocking collectives: 13.1 us -> 0 us
  local copies, waits for them, and re-layouts: 16.1 us -> 4.26 us
  other arithmetic: 11.8 us -> 0 us
    ppermute x5 -> x0, waiting for transfers between devices: 149 us -> none  [swapped(): lax.ppermute(value, axis, [(i, i ^ 1 << distance) for i in range(lax.axis...]
    pallas_call x0 -> x1, Pallas kernels: none -> 69.1 us  [per_device(): pl.pallas_call(kernel, out_shape=jax.ShapeDtypeStruct((H, T, D), BF16), i...]
    dot_general x11 -> x0, matrix products: 53.4 us -> none  [the longest x8 23.4 us: per_device(): jnp.einsum('thd,hde->the', queries, buckets[bit_pos], preferred_element_t...]
    ppermute x5 -> x0, starting transfers between devices: 16.3 us -> none  [swapped(): lax.ppermute(value, axis, [(i, i ^ 1 << distance) for i in range(lax.axis...]
    all_gather x1 -> x0, blocking collectives: 13.1 us -> none  [per_device(): states = lax.all_gather(share_rows[None], 'outer', axis=0, tiled=True)]
    unnamed x33 -> x0, local copies, waits for them, and re-layouts: 9.34 us -> none
    all_to_all x1 -> x0, starting transfers between devices: 8.79 us -> none  [sent_to_all(): return lax.all_to_all(copies, axis, split_axis=0, concat_axis=0, tiled=True)]
    eq x5 -> x0, other arithmetic: 5.45 us -> none  [local_terms(): levels_at == level_idx]
  transfers between devices with their start and end apart: 6 -> 0, of which waited for: 6 -> 0; matrix products, arithmetic and copies ran while one was open for 18% -> 0% of each run, Pallas kernels for 0% -> 0%
where the time goes in v1:
time: 74.5 us; the launch traced here: 73.4 us
  Pallas kernels  69.1 us (93%)
  local copies, waits for them, and re-layouts  4.26 us (6%)
    pallas_call x1, Pallas kernels, per_device(): pl.pallas_call(kernel, out_shape=jax.ShapeDtypeStruct((H, T, D), BF16), i...  69.1 us
    transpose x1, local copies, waits for them, and re-layouts, per_device(): return jnp.transpose(by_head, (1, 0, 2))  4.26 us

profile of v1, /device:TPU:8, one launch (start us, length us, event | category | flops | bytes accessed | tf_op | source)
XLA Modules:
  0.0 73.4 jit_solution(6141979638920659741)
XLA Ops:
  0.0 69.1 %shard_map.46 = bf16[16,512,128]{2,1,0:T(8,128)(2,1)} custom-call(bf16[512,16,128]{2,1,0:T(8,128)(2,1)} %q_hbm.1, bf16[512,16,128]{2,1,0:T(8,128)(2,1)} %k_hbm.1, bf16[512,16,128]{2,1,0:T(8,128)(2,1)} %v_hbm.1, f32[18,16,512]{2,1,0:T(8,128)} %lw_hbm.1), custom_call_target="tpu_custom_call" | custom-call | tf_op jit(solution)/shard_map/pallas_call | solution.py:283
  69.1 4.3 %copy.5 = bf16[512,16,128]{2,1,0:T(8,128)(2,1)} copy(bf16[512,16,128]{2,0,1:T(8,128)(2,1)} %bitcast.1) | data formatting | bytes 4194304 | tf_op jit(solution)/shard_map/transpose | solution.py:315

commit v2 on v1

--- a/solution.py
+++ b/solution.py
@@ -18,9 +18,11 @@
 LEVELS = 18
 LOCAL_BITS = 9
 TILE = 128
-HOP = 2
-DELAY = [HOP * tier for tier in range(TIERS + 1)]
-TICKS = H + DELAY[TIERS]
+STAGES = 6
+SLOTS = 10
+DELAY = [0, 3, 6, 9, 12, 14, 17]
+LOCAL_AT = 0
+TICKS = H + DELAY[STAGES]
 FACTOR = [2.0 ** (-0.5 * level) for level in range(LEVELS)]
 
 
@@ -40,9 +42,9 @@
 
 
 def kernel(
-    q_hbm, k_hbm, v_hbm, lw_hbm, o_hbm,
-    x_in, k_in, v_in, lw, q32, k32, v32, qh, kh, vt, wt, acc, outs,
-    run, sent, got, in_sem, out_sem, send_sem, extra_sem, recv_sem,
+    q_hbm, k_hbm, v_hbm, lw_hbm, out,
+    x_in, k_in, v_in, lw, q32, k32, v32, qh, kh, vt, wt, acc,
+    run, sent, got, in_sem, send_sem, recv_sem,
 ):
     outer = lax.axis_index("outer")
     inner = lax.axis_index("inner")
@@ -76,45 +78,66 @@
     second2 = jnp.where(z == 0, 6, jnp.where(z == 7, 1, jnp.where(z == 3, 5, 2)))
     serves2 = either(z, 0, 3, 4, 7)
 
-    partner = [
-        at(flip(z), x, y, core),
-        at(source1, x, y, core),
-        at(source2, x, y, core),
-        at(z, flip(x), y, core),
-        at(z, 3 - x, y, core),
-        at(z, x, y, 1 - core),
-        at(z, x, flip(y), core),
-        at(z, x, 3 - y, core),
+    far_y = lax.rem(y + 2, 4)
+    far_x = lax.rem(x + 2, 4)
+    routes = [
+        [(0, at(flip(z), x, y, core), None)],
+        [(1, at(second1, x, y, core), serves1), (1, at(source1, x, y, core), serves1)],
+        [(2, at(second2, x, y, core), serves2), (2, at(source2, x, y, core), serves2)],
+        [(4, at(z, far_x, y, core), None), (3, at(z, flip(x), y, core), None), (8, at(z, 3 - x, y, core), None)],
+        [(5, at(z, x, y, 1 - core), None)],
+        [(7, at(z, x, far_y, core), None), (6, at(z, x, flip(y), core), None), (9, at(z, x, 3 - y, core), None)],
     ]
-    second = {1: at(second1, x, y, core), 2: at(second2, x, y, core)}
-    serves = {1: serves1, 2: serves2}
+    arrivals = [[0], [1], [2], [3, 4, 8], [5], [6, 7, 9]]
+
+    def guarded(condition, action):
+        if condition is None:
+            action()
+        else:
+            pl.when(condition)(action)
+
+    def greet(device):
+        pl.semaphore_signal(barrier, inc=1, device_id=device, device_id_type=MESH)
 
     barrier = pltpu.get_barrier_semaphore()
-    for tier in range(TIERS):
-        pl.semaphore_signal(barrier, inc=1, device_id=partner[tier], device_id_type=MESH)
-    for tier in (1, 2):
-        @pl.when(serves[tier])
-        def _(tier=tier):
-            pl.semaphore_signal(barrier, inc=1, device_id=second[tier], device_id_type=MESH)
-
-    def send(tier, c, device, sem):
+    for stage in (0, 3, 4, 5):
+        for _slot, device, _who in routes[stage]:
+            greet(device)
+    for stage in (1, 2):
+        far, near = routes[stage]
+        greet(near[1])
+        guarded(far[2], lambda far=far: greet(far[1]))
+
+    number = {}
+    for stage in range(STAGES):
+        for index in range(len(routes[stage])):
+            number[stage, index] = len(number)
+
+    def send(stage, index, c):
+        slot, device, _who = routes[stage][index]
         return pltpu.make_async_remote_copy(
-            src_ref=sent.at[tier, c],
-            dst_ref=got.at[tier, c],
-            send_sem=sem,
-            recv_sem=recv_sem.at[tier, c],
+            src_ref=sent.at[stage, c],
+            dst_ref=got.at[slot, c],
+            send_sem=send_sem.at[number[stage, index]],
+            recv_sem=recv_sem.at[slot, c],
             device_id=device,
             device_id_type=MESH,
         )
 
-    def start_sends(tier, c):
-        if tier in serves:
-            @pl.when(serves[tier])
-            def _():
-                send(tier, c, partner[tier], send_sem.at[tier]).start()
-                send(tier, c, second[tier], extra_sem.at[tier]).start()
-        else:
-            send(tier, c, partner[tier], send_sem.at[tier]).start()
+    def start_sends(stage, c):
+        for index, (_slot, _device, who) in enumerate(routes[stage]):
+            guarded(who, lambda index=index: send(stage, index, c).start())
+
+    def receive(stage, c):
+        for slot in arrivals[stage]:
+            pltpu.make_async_remote_copy(
+                src_ref=sent.at[stage, c],
+                dst_ref=got.at[slot, c],
+                send_sem=send_sem.at[0],
+                recv_sem=recv_sem.at[slot, c],
+                device_id=routes[stage][0][1],
+                device_id_type=MESH,
+            ).wait_recv()
 
     def widen(source, target):
         def step(i, carry):
@@ -133,7 +156,7 @@
     wt[pl.ds(TILE, TILE), pl.ds(0, TILE)] = jnp.zeros((TILE, TILE), BF16)
     wt[pl.ds(3 * TILE, TILE), pl.ds(2 * TILE, TILE)] = jnp.zeros((TILE, TILE), BF16)
 
-    waits = 8 + serves1.astype(jnp.int32) + serves2.astype(jnp.int32)
+    waits = 10 + serves1.astype(jnp.int32) + serves2.astype(jnp.int32)
     pl.semaphore_wait(barrier, waits)
 
     lane = lax.rem(lax.broadcasted_iota(jnp.int32, (16, T), 1), TILE)
@@ -193,6 +216,8 @@
 
     def finish(c):
         half = T // 2
+        buckets = [got[tier, c] for tier in range(TIERS - 1)]
+        buckets.append((got[7, c].astype(F32) + got[9, c].astype(F32)).astype(BF16))
         for part in range(2):
             cols = pl.ds(part * half, half)
             q = qh[c, pl.ds(part * half, half), :]
@@ -201,12 +226,11 @@
                 row = lw[LOCAL_BITS + 1 + tier, pl.ds(c, 1), cols] * (
                     switches[tier] * FACTOR[LOCAL_BITS + 1 + tier]
                 )
-                total = total + dot_nt(got[tier, c], q) * row
-            outs[c, pl.ds(part * half, half), :] = total.T.astype(BF16)
-        pltpu.make_async_copy(outs.at[c], o_hbm.at[c], out_sem.at[c]).start()
-
-    def active(t, tier):
-        return jnp.logical_and(t >= DELAY[tier], t < DELAY[tier] + H)
+                total = total + dot_nt(buckets[tier], q) * row
+            out[pl.ds(part * half * H + c, half, stride=H), :] = total.T
+
+    def active(t, start):
+        return jnp.logical_and(t >= start, t < start + H)
 
     def tick(t, carry):
         @pl.when(active(t, 0))
@@ -219,72 +243,64 @@
             run[t] = state
             sent[0, t] = state.astype(BF16)
 
-        for tier in range(1, TIERS):
-            @pl.when(active(t, tier))
-            def _(tier=tier):
-                c = t - DELAY[tier]
-                send(tier - 1, c, partner[tier - 1], send_sem.at[tier - 1]).wait_recv()
-                total = run[c] + got[tier - 1, c].astype(F32)
+        for stage in range(1, STAGES):
+            @pl.when(active(t, DELAY[stage]))
+            def _(stage=stage):
+                c = t - DELAY[stage]
+                receive(stage - 1, c)
+                if stage == 4:
+                    other = got[4, c].astype(F32) + got[8, c].astype(F32)
+                    got[4, c] = other.astype(BF16)
+                    total = run[c] + got[3, c].astype(F32) + other
+                else:
+                    total = run[c] + got[arrivals[stage - 1][0], c].astype(F32)
                 run[c] = total
-                sent[tier, c] = total.astype(BF16)
-
-        for tier in range(TIERS):
-            @pl.when(active(t, tier))
-            def _(tier=tier):
-                start_sends(tier, t - DELAY[tier])
-
-        @pl.when(active(t, 0))
+                sent[stage, c] = total.astype(BF16)
+
+        for stage in range(STAGES):
+            @pl.when(active(t, DELAY[stage]))
+            def _(stage=stage):
+                start_sends(stage, t - DELAY[stage])
+
+        @pl.when(active(t, LOCAL_AT))
         def _():
-            @pl.when(t == 0)
+            @pl.when(t == LOCAL_AT)
             def _():
                 copies[2].wait()
                 copies[3].wait()
                 widen(x_in, q32)
-            local(t)
-
-        @pl.when(active(t, TIERS))
+            local(t - LOCAL_AT)
+
+        @pl.when(active(t, DELAY[STAGES]))
         def _():
-            c = t - DELAY[TIERS]
-            send(TIERS - 1, c, partner[TIERS - 1], send_sem.at[TIERS - 1]).wait_recv()
+            c = t - DELAY[STAGES]
+            receive(STAGES - 1, c)
             finish(c)
 
         return carry
 
     lax.fori_loop(0, TICKS, tick, 0)
 
-    def whole(tier, device, sem):
-        return pltpu.make_async_remote_copy(
-            src_ref=sent.at[tier],
-            dst_ref=got.at[tier],
-            send_sem=sem,
-            recv_sem=recv_sem.at[tier, 0],
-            device_id=device,
-            device_id_type=MESH,
-        )
-
-    for tier in range(TIERS):
-        if tier in serves:
-            @pl.when(serves[tier])
-            def _(tier=tier):
-                whole(tier, partner[tier], send_sem.at[tier]).wait_send()
-                whole(tier, second[tier], extra_sem.at[tier]).wait_send()
-        else:
-            whole(tier, partner[tier], send_sem.at[tier]).wait_send()
-
-    def drain(c, carry):
-        pltpu.make_async_copy(outs.at[c], o_hbm.at[c], out_sem.at[c]).wait()
-        return carry
-
-    lax.fori_loop(0, H, drain, 0)
+    for stage in range(STAGES):
+        for index, (slot, device, who) in enumerate(routes[stage]):
+            whole = pltpu.make_async_remote_copy(
+                src_ref=sent.at[stage],
+                dst_ref=got.at[slot],
+                send_sem=send_sem.at[number[stage, index]],
+                recv_sem=recv_sem.at[slot, 0],
+                device_id=device,
+                device_id_type=MESH,
+            )
+            guarded(who, whole.wait_send)
 
 
 def per_device(queries, key_vectors, value_vectors, level_weights):
-    hbm = pl.BlockSpec(memory_space=pl.ANY)
-    by_head = pl.pallas_call(
+    hbm = pl.BlockSpec(memory_space=pltpu.HBM)
+    summed = pl.pallas_call(
         kernel,
-        out_shape=jax.ShapeDtypeStruct((H, T, D), BF16),
+        out_shape=pltpu.VMEM((T * H, D), F32),
         in_specs=[hbm] * 4,
-        out_specs=hbm,
+        out_specs=pl.BlockSpec(memory_space=pltpu.VMEM),
         scratch_shapes=[
             pltpu.VMEM((T, H, D), BF16),
             pltpu.VMEM((T, H, D), BF16),
@@ -298,21 +314,18 @@
             pltpu.VMEM((H, D, T), BF16),
             pltpu.VMEM((T, T), BF16),
             pltpu.VMEM((H, D, T), F32),
-            pltpu.VMEM((H, T, D), BF16),
             pltpu.VMEM((H, D, D), F32),
-            pltpu.VMEM((TIERS, H, D, D), BF16),
-            pltpu.VMEM((TIERS, H, D, D), BF16),
+            pltpu.VMEM((STAGES, H, D, D), BF16),
+            pltpu.VMEM((SLOTS, H, D, D), BF16),
             pltpu.SemaphoreType.DMA((4,)),
-            pltpu.SemaphoreType.DMA((H,)),
-            pltpu.SemaphoreType.DMA((TIERS,)),
-            pltpu.SemaphoreType.DMA((TIERS,)),
-            pltpu.SemaphoreType.DMA((TIERS, H)),
+            pltpu.SemaphoreType.DMA((12,)),
+            pltpu.SemaphoreType.DMA((SLOTS, H)),
         ],
         compiler_params=pltpu.CompilerParams(
-            collective_id=0, has_side_effects=True, vmem_limit_bytes=60 * 1024 * 1024
+            collective_id=0, has_side_effects=True, vmem_limit_bytes=62_400_000
         ),
     )(queries, key_vectors, value_vectors, level_weights)
-    return jnp.transpose(by_head, (1, 0, 2))
+    return summed.reshape(T, H, D).astype(BF16)
 
 
 def solution(mesh):

time: 74.5 us -> 57 us (0.77)
  the two profiles are of different devices: /device:TPU:8 before, /device:TPU:1 now
where the time goes in v2:
time: 57 us
  Pallas kernels  55.4 us (97%)
  other arithmetic  1.52 us (3%)
    pallas_call x1, Pallas kernels, per_device(): pl.pallas_call(kernel, out_shape=pltpu.VMEM((T * H, D), F32), in_specs=[h...  55.4 us
    convert_element_type x1, other arithmetic, per_device(): return summed.reshape(T, H, D).astype(BF16)  1.52 us

profile of v2, /device:TPU:1, one launch (start us, length us, event | category | flops | bytes accessed | tf_op | source)
XLA Modules:
  0.0 57.0 jit_solution(2571496680359319076)
XLA Ops:
  0.0 55.4 %shard_map.46 = f32[8192,128]{1,0:T(8,128)S(1)} custom-call(bf16[512,16,128]{2,1,0:T(8,128)(2,1)} %q_hbm.1, bf16[512,16,128]{2,1,0:T(8,128)(2,1)} %k_hbm.1, bf16[512,16,128]{2,1,0:T(8,128)(2,1)} %v_hbm.1, f32[18,16,512]{2,1,0:T(8,128)} %lw_hbm.1), custom_call_target="tpu_custom_call" | custom-call | tf_op jit(solution)/shard_map/pallas_call | solution.py:299
  55.4 1.5 %convert_element_type.6 = bf16[8192,128]{1,0:T(8,128)(2,1)} convert(f32[8192,128]{1,0:T(8,128)S(1)} %shard_map.46) | non-fusion elementwise | flops 1048576 | bytes 6291456 | tf_op jit(solution)/shard_map/convert_element_type | solution.py:328

commit v3 on v2

--- a/solution.py
+++ b/solution.py
@@ -21,7 +21,8 @@
 STAGES = 6
 SLOTS = 10
 DELAY = [0, 3, 6, 9, 12, 14, 17]
-LOCAL_AT = 0
+LOCAL_AT = 2
+STRIP = 64
 TICKS = H + DELAY[STAGES]
 FACTOR = [2.0 ** (-0.5 * level) for level in range(LEVELS)]
 
@@ -43,8 +44,8 @@
 
 def kernel(
     q_hbm, k_hbm, v_hbm, lw_hbm, out,
-    x_in, k_in, v_in, lw, q32, k32, v32, qh, kh, vt, wt, acc,
-    run, sent, got, in_sem, send_sem, recv_sem,
+    x_in, k_in, v_in, lw, qh, kh, vh, vt, wt, acc, heads,
+    run, sent, got, in_sem, key_sem, value_sem, send_sem, recv_sem,
 ):
     outer = lax.axis_index("outer")
     inner = lax.axis_index("inner")
@@ -55,12 +56,22 @@
     p = lax.rem(z, 4)
     place = outer * 32 + inner
 
+    def strip(i):
+        return pl.ds(pl.multiple_of(i * STRIP, STRIP), STRIP)
+
+    def key_copy(i):
+        return pltpu.make_async_copy(k_hbm.at[strip(i)], k_in.at[strip(i)], key_sem.at[i])
+
+    def value_copy(i):
+        return pltpu.make_async_copy(v_hbm.at[strip(i)], v_in.at[strip(i)], value_sem.at[i])
+
     copies = [
-        pltpu.make_async_copy(k_hbm, k_in, in_sem.at[0]),
-        pltpu.make_async_copy(v_hbm, v_in, in_sem.at[1]),
-        pltpu.make_async_copy(lw_hbm, lw, in_sem.at[2]),
-        pltpu.make_async_copy(q_hbm, x_in, in_sem.at[3]),
+        pltpu.make_async_copy(lw_hbm, lw, in_sem.at[0]),
+        pltpu.make_async_copy(q_hbm, x_in, in_sem.at[1]),
     ]
+    for i in range(T // STRIP):
+        key_copy(i).start()
+        value_copy(i).start()
     for copy in copies:
         copy.start()
 
@@ -79,6 +90,9 @@
     serves2 = either(z, 0, 3, 4, 7)
 
     far_y = lax.rem(y + 2, 4)
+    low_y = y < 2
+    even_y = lax.rem(y, 2) == 0
+    taken = {6: jnp.logical_not(even_y), 7: jnp.logical_not(low_y), 9: jnp.logical_not(low_y)}
     far_x = lax.rem(x + 2, 4)
     routes = [
         [(0, at(flip(z), x, y, core), None)],
@@ -86,7 +100,7 @@
         [(2, at(second2, x, y, core), serves2), (2, at(source2, x, y, core), serves2)],
         [(4, at(z, far_x, y, core), None), (3, at(z, flip(x), y, core), None), (8, at(z, 3 - x, y, core), None)],
         [(5, at(z, x, y, 1 - core), None)],
-        [(7, at(z, x, far_y, core), None), (6, at(z, x, flip(y), core), None), (9, at(z, x, 3 - y, core), None)],
+        [(7, at(z, x, far_y, core), low_y), (6, at(z, x, flip(y), core), even_y), (9, at(z, x, 3 - y, core), low_y)],
     ]
     arrivals = [[0], [1], [2], [3, 4, 8], [5], [6, 7, 9]]
 
@@ -130,29 +144,35 @@
 
     def receive(stage, c):
         for slot in arrivals[stage]:
-            pltpu.make_async_remote_copy(
+            copy = pltpu.make_async_remote_copy(
                 src_ref=sent.at[stage, c],
                 dst_ref=got.at[slot, c],
                 send_sem=send_sem.at[0],
                 recv_sem=recv_sem.at[slot, c],
                 device_id=routes[stage][0][1],
                 device_id_type=MESH,
-            ).wait_recv()
-
-    def widen(source, target):
-        def step(i, carry):
-            rows = source[pl.ds(i * 32, 32)].astype(F32).reshape(32 * H, D)
-            target[pl.ds(pl.multiple_of(i * 32 * H, 32 * H), 32 * H), :] = rows
-            return carry
-        lax.fori_loop(0, T // 32, step, 0)
-
-    def head_of(source, c):
-        return source[pl.ds(c, T, stride=H), :].astype(BF16)
-
-    copies[0].wait()
-    widen(k_in, k32)
-    copies[1].wait()
-    widen(v_in, v32)
+            )
+            guarded(taken.get(slot), copy.wait_recv)
+
+    def by_head(source, target, i):
+        target[:, strip(i), :] = jnp.transpose(source[strip(i)], (1, 0, 2))
+
+    def unpack_keys_values(i, carry):
+        key_copy(i).wait()
+        by_head(k_in, kh, i)
+        value_copy(i).wait()
+        by_head(v_in, vh, i)
+        return carry
+
+    def unpack_queries(i, carry):
+        by_head(x_in, qh, i)
+        return carry
+
+    lax.fori_loop(0, T // STRIP, unpack_keys_values, 0)
+    for slot, who in taken.items():
+        @pl.when(jnp.logical_not(who))
+        def _(slot=slot):
+            got[slot] = jnp.zeros((H, D, D), BF16)
     wt[pl.ds(TILE, TILE), pl.ds(0, TILE)] = jnp.zeros((TILE, TILE), BF16)
     wt[pl.ds(3 * TILE, TILE), pl.ds(2 * TILE, TILE)] = jnp.zeros((TILE, TILE), BF16)
 
@@ -171,8 +191,7 @@
         return lw[level, pl.ds(c, 1), :] * FACTOR[level]
 
     def local(c):
-        q = head_of(q32, c)
-        qh[c] = q
+        q = qh[c]
         keys = kh[c]
         wide = jnp.zeros((16, T), F32)
         for level in (4, 5, 6, 7):
@@ -227,7 +246,7 @@
                     switches[tier] * FACTOR[LOCAL_BITS + 1 + tier]
                 )
                 total = total + dot_nt(buckets[tier], q) * row
-            out[pl.ds(part * half * H + c, half, stride=H), :] = total.T
+            heads[c, pl.ds(part * half, half), :] = total.astype(BF16).T
 
     def active(t, start):
         return jnp.logical_and(t >= start, t < start + H)
@@ -235,15 +254,13 @@
     def tick(t, carry):
         @pl.when(active(t, 0))
         def _():
-            keys = head_of(k32, t)
-            kh[t] = keys
-            values = v32[pl.ds(t, T, stride=H), :].T.astype(BF16)
+            values = vh[t].T
             vt[t] = values
-            state = dot_nn(values, keys)
+            state = dot_nn(values, kh[t])
             run[t] = state
             sent[0, t] = state.astype(BF16)
 
-        for stage in range(1, STAGES):
+        for stage in reversed(range(1, STAGES)):
             @pl.when(active(t, DELAY[stage]))
             def _(stage=stage):
                 c = t - DELAY[stage]
@@ -257,7 +274,7 @@
                 run[c] = total
                 sent[stage, c] = total.astype(BF16)
 
-        for stage in range(STAGES):
+        for stage in (4, 5, 3, 2, 1, 0):
             @pl.when(active(t, DELAY[stage]))
             def _(stage=stage):
                 start_sends(stage, t - DELAY[stage])
@@ -266,9 +283,9 @@
         def _():
             @pl.when(t == LOCAL_AT)
             def _():
-                copies[2].wait()
-                copies[3].wait()
-                widen(x_in, q32)
+                copies[0].wait()
+                copies[1].wait()
+                lax.fori_loop(0, T // STRIP, unpack_queries, 0)
             local(t - LOCAL_AT)
 
         @pl.when(active(t, DELAY[STAGES]))
@@ -280,6 +297,12 @@
         return carry
 
     lax.fori_loop(0, TICKS, tick, 0)
+
+    def by_position(i, carry):
+        out[strip(i)] = jnp.transpose(heads[:, strip(i), :], (1, 0, 2))
+        return carry
+
+    lax.fori_loop(0, T // STRIP, by_position, 0)
 
     for stage in range(STAGES):
         for index, (slot, device, who) in enumerate(routes[stage]):
@@ -296,9 +319,9 @@
 
 def per_device(queries, key_vectors, value_vectors, level_weights):
     hbm = pl.BlockSpec(memory_space=pltpu.HBM)
-    summed = pl.pallas_call(
+    return pl.pallas_call(
         kernel,
-        out_shape=pltpu.VMEM((T * H, D), F32),
+        out_shape=pltpu.VMEM((T, H, D), BF16),
         in_specs=[hbm] * 4,
         out_specs=pl.BlockSpec(memory_space=pltpu.VMEM),
         scratch_shapes=[
@@ -306,26 +329,26 @@
             pltpu.VMEM((T, H, D), BF16),
             pltpu.VMEM((T, H, D), BF16),
             pltpu.VMEM((LEVELS, H, T), F32),
-            pltpu.VMEM((T * H, D), F32),
-            pltpu.VMEM((T * H, D), F32),
-            pltpu.VMEM((T * H, D), F32),
+            pltpu.VMEM((H, T, D), BF16),
             pltpu.VMEM((H, T, D), BF16),
             pltpu.VMEM((H, T, D), BF16),
             pltpu.VMEM((H, D, T), BF16),
             pltpu.VMEM((T, T), BF16),
             pltpu.VMEM((H, D, T), F32),
+            pltpu.VMEM((H, T, D), BF16),
             pltpu.VMEM((H, D, D), F32),
             pltpu.VMEM((STAGES, H, D, D), BF16),
             pltpu.VMEM((SLOTS, H, D, D), BF16),
-            pltpu.SemaphoreType.DMA((4,)),
+            pltpu.SemaphoreType.DMA((2,)),
+            pltpu.SemaphoreType.DMA((T // STRIP,)),
+            pltpu.SemaphoreType.DMA((T // STRIP,)),
             pltpu.SemaphoreType.DMA((12,)),
             pltpu.SemaphoreType.DMA((SLOTS, H)),
         ],
         compiler_params=pltpu.CompilerParams(
-            collective_id=0, has_side_effects=True, vmem_limit_bytes=62_400_000
+            collective_id=0, has_side_effects=True, vmem_limit_bytes=64_500_000
         ),
     )(queries, key_vectors, value_vectors, level_weights)
-    return summed.reshape(T, H, D).astype(BF16)
 
 
 def solution(mesh):

time: 57 us -> 55.1 us (0.967)
  the two profiles are of different devices: /device:TPU:1 before, /device:TPU:8 now
where the time goes in v3:
time: 55.1 us; the launch traced here: 54.9 us
  Pallas kernels  53.6 us (97%)
  local copies, waits for them, and re-layouts  1.32 us (2%)
    pallas_call x1, Pallas kernels, per_device(): pl.pallas_call(kernel, out_shape=pltpu.VMEM((T, H, D), BF16), in_specs=[h...  53.6 us
    unnamed x1, local copies, waits for them, and re-layouts  1.32 us

profile of v3, /device:TPU:8, one launch (start us, length us, event | category | flops | bytes accessed | tf_op | source)
XLA Modules:
  0.0 54.9 jit_solution(618402096633149660)
XLA Ops:
  0.0 53.6 %shard_map.46 = bf16[512,16,128]{2,1,0:T(8,128)(2,1)S(1)} custom-call(bf16[512,16,128]{2,1,0:T(8,128)(2,1)} %q_hbm.1, bf16[512,16,128]{2,1,0:T(8,128)(2,1)} %k_hbm.1, bf16[512,16,128]{2,1,0:T(8,128)(2,1)} %v_hbm.1, f32[18,16,512]{2,1,0:T(8,128)} %lw_hbm.1), custom_call_target="tpu_custom_call" | custom-call | tf_op jit(solution)/shard_map/pallas_call | solution.py:322
  53.6 1.3 %copy.6 = bf16[512,16,128]{2,1,0:T(8,128)(2,1)} copy(bf16[512,16,128]{2,1,0:T(8,128)(2,1)S(1)} %shard_map.46) | data formatting | bytes 4194304

commit v4 on v3

--- a/solution.py
+++ b/solution.py
@@ -20,9 +20,10 @@
 TILE = 128
 STAGES = 6
 SLOTS = 10
-DELAY = [0, 3, 6, 9, 12, 14, 17]
-LOCAL_AT = 2
+DELAY = [0, 3, 6, 9, 12, 13, 16]
+LOCAL_AT = 3
 STRIP = 64
+HALF = 8
 TICKS = H + DELAY[STAGES]
 FACTOR = [2.0 ** (-0.5 * level) for level in range(LEVELS)]
 
@@ -72,8 +73,6 @@
     for i in range(T // STRIP):
         key_copy(i).start()
         value_copy(i).start()
-    for copy in copies:
-        copy.start()
 
     def flip(value):
         return value + 1 - 2 * lax.rem(value, 2)
@@ -169,6 +168,8 @@
         return carry
 
     lax.fori_loop(0, T // STRIP, unpack_keys_values, 0)
+    for copy in copies:
+        copy.start()
     for slot, who in taken.items():
         @pl.when(jnp.logical_not(who))
         def _(slot=slot):
@@ -251,6 +252,15 @@
     def active(t, start):
         return jnp.logical_and(t >= start, t < start + H)
 
+    def by_position(half):
+        some = pl.ds(half * HALF, HALF)
+
+        def step(i, carry):
+            out[strip(i), some, :] = jnp.transpose(heads[some, strip(i), :], (1, 0, 2))
+            return carry
+
+        lax.fori_loop(0, T // STRIP, step, 0)
+
     def tick(t, carry):
         @pl.when(active(t, 0))
         def _():
@@ -294,15 +304,15 @@
             receive(STAGES - 1, c)
             finish(c)
 
+        @pl.when(t == DELAY[STAGES] + HALF)
+        def _():
+            by_position(0)
+
         return carry
 
     lax.fori_loop(0, TICKS, tick, 0)
 
-    def by_position(i, carry):
-        out[strip(i)] = jnp.transpose(heads[:, strip(i), :], (1, 0, 2))
-        return carry
-
-    lax.fori_loop(0, T // STRIP, by_position, 0)
+    by_position(1)
 
     for stage in range(STAGES):
         for index, (slot, device, who) in enumerate(routes[stage]):

time: 55.1 us -> 54 us (0.980)
  Pallas kernels: 53.6 us -> 52.5 us
    pallas_call x1, Pallas kernels: 53.6 us -> 52.5 us  [per_device(): pl.pallas_call(kernel, out_shape=pltpu.VMEM((T, H, D), BF16), in_specs=[h...]
where the time goes in v4:
time: 54 us; the launch traced here: 53.9 us
  Pallas kernels  52.5 us (97%)
  local copies, waits for them, and re-layouts  1.32 us (2%)
    pallas_call x1, Pallas kernels, per_device(): pl.pallas_call(kernel, out_shape=pltpu.VMEM((T, H, D), BF16), in_specs=[h...  52.5 us
    unnamed x1, local copies, waits for them, and re-layouts  1.32 us

profile of v4, /device:TPU:8, one launch (start us, length us, event | category | flops | bytes accessed | tf_op | source)
XLA Modules:
  0.0 53.9 jit_solution(8079231356047477721)
XLA Ops:
  0.0 52.5 %shard_map.46 = bf16[512,16,128]{2,1,0:T(8,128)(2,1)S(1)} custom-call(bf16[512,16,128]{2,1,0:T(8,128)(2,1)} %q_hbm.1, bf16[512,16,128]{2,1,0:T(8,128)(2,1)} %k_hbm.1, bf16[512,16,128]{2,1,0:T(8,128)(2,1)} %v_hbm.1, f32[18,16,512]{2,1,0:T(8,128)} %lw_hbm.1), custom_call_target="tpu_custom_call" | custom-call | tf_op jit(solution)/shard_map/pallas_call | solution.py:332
  52.5 1.3 %copy.6 = bf16[512,16,128]{2,1,0:T(8,128)(2,1)} copy(bf16[512,16,128]{2,1,0:T(8,128)(2,1)S(1)} %shard_map.46) | data formatting | bytes 4194304

commit v5 on v4

--- a/solution.py
+++ b/solution.py
@@ -20,7 +20,7 @@
 TILE = 128
 STAGES = 6
 SLOTS = 10
-DELAY = [0, 3, 6, 9, 12, 13, 16]
+DELAY = [0, 3, 6, 10, 13, 14, 17]
 LOCAL_AT = 3
 STRIP = 64
 HALF = 8

time: 54 us -> 54.7 us (1.013)
  no operation moved by 1% of the time
where the time goes in v5:
time: 54.7 us; the launch traced here: 54.3 us
  Pallas kernels  53 us (97%)
  local copies, waits for them, and re-layouts  1.32 us (2%)
    pallas_call x1, Pallas kernels, per_device(): pl.pallas_call(kernel, out_shape=pltpu.VMEM((T, H, D), BF16), in_specs=[h...  53 us
    unnamed x1, local copies, waits for them, and re-layouts  1.32 us

profile of v5, /device:TPU:8, one launch (start us, length us, event | category | flops | bytes accessed | tf_op | source)
XLA Modules:
  0.0 54.3 jit_solution(4598903275879173078)
XLA Ops:
  0.0 53.0 %shard_map.46 = bf16[512,16,128]{2,1,0:T(8,128)(2,1)S(1)} custom-call(bf16[512,16,128]{2,1,0:T(8,128)(2,1)} %q_hbm.1, bf16[512,16,128]{2,1,0:T(8,128)(2,1)} %k_hbm.1, bf16[512,16,128]{2,1,0:T(8,128)(2,1)} %v_hbm.1, f32[18,16,512]{2,1,0:T(8,128)} %lw_hbm.1), custom_call_target="tpu_custom_call" | custom-call | tf_op jit(solution)/shard_map/pallas_call | solution.py:332
  53.0 1.3 %copy.6 = bf16[512,16,128]{2,1,0:T(8,128)(2,1)} copy(bf16[512,16,128]{2,1,0:T(8,128)(2,1)S(1)} %shard_map.46) | data formatting | bytes 4194304
